TPU v7x, 32 devices: a whole 2x2x4 slice. The times are simulated.
32 devices in a mesh: grp: 2 (over core), slab: 4 (over z), col: 4 (over y, x).
Axes of the slice: x: 2, y: 2, z: 4, core: 2. Of those that a mesh axis runs over, the one named last changes fastest.
Arguments:
- solution: float32 [512, 8192], P('slab', ('grp', 'col')), may hold values from -6 to 6
- residual: float32 [512, 8192], P('slab', ('grp', 'col')), may hold values from -0.6 to 0.6
- direction: float32 [512, 8192], P('slab', ('grp', 'col')), may hold values from -6 to 6
- row_taps: float32 [31], replicated, may hold values from 0.2 to 1
- col_taps: float32 [31], replicated, may hold values from 0.2 to 1
- damping: float32 [], replicated, may hold values from 0.01 to 0.05
- rho: float32 [], replicated, may hold values from 83886.08 to 251658.23
- coarse_diag: float32 [4], replicated, may hold values from 0.9 to 1.6
- coarse_coupling: float32 [4], replicated, may hold values from 0.05 to 0.2
Outputs:
- new_solution: float32 [512, 8192], P('slab', ('grp', 'col'))
- new_residual: float32 [512, 8192], P('slab', ('grp', 'col'))
- precond: float32 [512, 8192], P('slab', ('grp', 'col'))
- new_direction: float32 [512, 8192], P('slab', ('grp', 'col'))
- energy: float32 [], replicated
All inputs are finite; a program needn't handle non-finite values.
Results may differ from a plain program's by a relative error of at most 0.0001.
Values sent between devices are 32-bit elements; how exact they have to be, the bound alone decides.
A program may use at most 128 MiB of HBM per device.

v0:
```python
import functools

import jax
import jax.numpy as jnp
from jax import lax
from jax.experimental import pallas as pl
from jax.experimental.pallas import tpu as pltpu
from jax.sharding import PartitionSpec as P

SWEEPS = 3
LEVELS = 4
COARSE_SWEEPS = 4
RELAX = 2.0 / 3.0
HR = 32
HC = 128
BLK = 256
MESH = pl.DeviceIdType.MESH
F32 = jnp.float32
BF16 = jnp.bfloat16
DIRS = [(0, -1), (0, 1), (-1, 0), (1, 0), (-1, -1), (-1, 1), (1, -1), (1, 1)]


def split(x):
    hi = x.astype(BF16)
    return hi, (x - hi.astype(F32)).astype(BF16)


def dot(a, b):
    return jnp.dot(a, b, preferred_element_type=F32)


def dot_left(sel, x):
    hi, lo = split(x)
    return dot(sel, hi) + dot(sel, lo)


def dot_right(x, sel):
    hi, lo = split(x)
    return dot(hi, sel) + dot(lo, sel)


def iota(shape, dim):
    return lax.broadcasted_iota(jnp.int32, shape, dim)


def select(condition, value=1.0):
    return jnp.where(condition, F32(value), F32(0.0)).astype(BF16)


def lanes(n):
    return -(-n // 128) * 128


def fold(x):
    rows, cols = x.shape
    total = x.reshape(rows // 8, 8, cols).sum(axis=0)
    out = total[:, :128]
    for b in range(1, cols // 128):
        out = out + total[:, 128 * b : 128 * b + 128]
    return out


def beside(v):
    rows, cols = v.shape
    i = iota(v.shape, 0)
    up = jnp.where(i == 0, 0.0, pltpu.roll(v, 1, 0))
    down = jnp.where(i == rows - 1, 0.0, pltpu.roll(v, rows - 1, 0))
    return up + down + pltpu.roll(v, 1, 1) + pltpu.roll(v, cols - 1, 1)


def kernel(
    sizes,
    sol_in,
    res_in,
    dir_in,
    row_taps,
    col_taps,
    damping,
    rho,
    diag,
    coupling,
    sol_out,
    res_out,
    pre_out,
    ndir_out,
    energy_out,
    fields,
    band,
    mc_hi,
    mc_lo,
    mr_hi,
    mr_lo,
    t_hi,
    t_lo,
    sum4,
    spread4,
    sol_buf,
    pre_buf,
    ndir_buf,
    rhs1,
    plane_sum,
    slab_sum,
    local_sem,
    out_sem,
    send_sem,
    recv_sem,
    gsend_sem,
    grecv_sem,
    psend_sem,
    precv_sem,
    ssend_sem,
    srecv_sem,
):
    H, W, n_slab, n_grp, n_col, taps = sizes
    n_lin = n_grp * n_col
    reach = taps // 2
    PH, PW = H + 2 * HR, W + 2 * HC
    slab = lax.axis_index("slab")
    lin = lax.axis_index("grp") * n_col + lax.axis_index("col")

    def device(s, l):
        return (l // n_col, s, l % n_col)

    def exists(dz, dc):
        s, l = slab + dz, lin + dc
        return (s >= 0) & (s < n_slab) & (l >= 0) & (l < n_lin)

    centre = (pl.ds(HR, H), pl.ds(HC, W))

    loads = [
        pltpu.make_async_copy(dir_in, fields.at[0].at[centre], local_sem.at[0]),
        pltpu.make_async_copy(res_in, fields.at[1].at[centre], local_sem.at[1]),
        pltpu.make_async_copy(sol_in, sol_buf, local_sem.at[2]),
    ]
    for load in loads:
        load.start()

    barrier = pltpu.get_barrier_semaphore()
    for i in range(1, n_lin):
        pl.semaphore_signal(
            barrier, inc=1, device_id=device(slab, (lin + i) % n_lin), device_id_type=MESH
        )
    for dc in (-1, 0, 1):

        @pl.when(exists(0, dc))
        def _():
            for i in range(1, n_slab):
                pl.semaphore_signal(
                    barrier,
                    inc=1,
                    device_id=device((slab + i) % n_slab, lin + dc),
                    device_id_type=MESH,
                )

    def side(d, halo, extent):
        return {-1: (0, halo), 0: (halo, extent), 1: (halo + extent, halo)}[d]

    for dz, dc in DIRS:
        r0, rn = side(dz, HR, H)
        c0, cn = side(dc, HC, W)

        @pl.when(jnp.logical_not(exists(dz, dc)))
        def _():
            for f in range(4):
                fields[f, r0 : r0 + rn, c0 : c0 + cn] = jnp.zeros((rn, cn), F32)

    W1 = W // 8
    H1 = H // 8
    for dc, c0 in ((-1, 0), (1, 2 * W1)):

        @pl.when(jnp.logical_not(exists(0, dc)))
        def _():
            rhs1[:, c0 : c0 + W1] = jnp.zeros((H1 * n_slab, W1), F32)

    near = 1 + (lin > 0).astype(jnp.int32) + (lin < n_lin - 1).astype(jnp.int32)
    pl.semaphore_wait(barrier, n_lin - 1 + (n_slab - 1) * near)

    def halo_copy(f, source, k):
        dz, dc = DIRS[k]

        def cut(d, halo, extent):
            src = {-1: (0, halo), 0: (0, extent), 1: (extent - halo, halo)}[d]
            dst = side(-d, halo, extent)[0]
            return src[0], dst, src[1]

        rs, rd, rn = cut(dz, HR, H)
        cs, cd, cn = cut(dc, HC, W)
        if source is None:
            src = fields.at[f, pl.ds(HR + rs, rn), pl.ds(HC + cs, cn)]
        else:
            src = source.at[pl.ds(rs, rn), pl.ds(cs, cn)]
        return pltpu.make_async_remote_copy(
            src_ref=src,
            dst_ref=fields.at[f, pl.ds(rd, rn), pl.ds(cd, cn)],
            send_sem=send_sem.at[f, k],
            recv_sem=recv_sem.at[f, k],
            device_id=device(slab + dz, lin + dc),
            device_id_type=MESH,
        )

    def halo_start(f, source=None):
        for k, (dz, dc) in enumerate(DIRS):

            @pl.when(exists(dz, dc))
            def _():
                halo_copy(f, source, k).start()

    def halo_arrive(f, source=None):
        for k, (dz, dc) in enumerate(DIRS):

            @pl.when(exists(-dz, -dc))
            def _():
                halo_copy(f, source, k).wait_recv()

    def halo_sent(f, source=None):
        for k, (dz, dc) in enumerate(DIRS):

            @pl.when(exists(dz, dc))
            def _():
                halo_copy(f, source, k).wait_send()

    halo_start(0, dir_in)
    halo_start(1, res_in)

    def banded(ref, first, rows, cols, offset):
        total = ref[0]
        for a in range(1, taps):
            total = total + ref[a]
        inverse = 1.0 / jnp.full((1, 1), total, F32)
        gap = iota((rows, cols), 1) - iota((rows, cols), 0) + (reach + offset - first)
        out = jnp.zeros((rows, cols), F32)
        for a in range(taps):
            out = jnp.where(gap == a, ref[a], out)
        return out * inverse

    def gram(c, keep):
        hi, lo = split(c)
        khi, klo = hi[:, keep], lo[:, keep]
        hit, lot = hi.T, lo.T
        return dot(hit, khi) + dot(lot, khi) + dot(hit, klo)

    for r in range(0, PH, 32):
        band[r : r + 32, 0:PH] = banded(row_taps, r, 32, PH, 0)
    m = iota((PH, PH), 0) + (slab * H - HR)
    c = jnp.where((m >= 0) & (m < H * n_slab), band[0:PH, 0:PH], 0.0)
    hi, lo = split(c)
    hit, lot = hi.T[HR : HR + H], lo.T[HR : HR + H]
    g = dot(hit, hi) + dot(lot, hi) + dot(hit, lo)
    ghi, glo = split(g)
    mr_hi[...] = ghi
    mr_lo[...] = glo

    WIN = BLK + 2 * HC
    band[...] = jnp.zeros((WIN, WIN), F32)
    for r in range(0, 128, 32):
        strip = banded(col_taps, r, 32, 384, -128)
        for b in range(WIN // 128):
            low = max(b - 1, 0)
            high = min(b + 2, WIN // 128)
            band[128 * b + r : 128 * b + r + 32, 128 * low : 128 * high] = strip[
                :, 128 * (low - b + 1) : 128 * (high - b + 1)
            ]
    blocks = W // BLK
    for v, j in ((0, 0), (1, None), (2, blocks - 1)):
        c = band[...]
        if j is not None:
            m = iota((WIN, WIN), 0) + (lin * W + BLK * j - HC)
            c = jnp.where((m >= 0) & (m < W * n_lin), c, 0.0)
        ghi, glo = split(gram(c, slice(HC, HC + BLK)))
        mc_hi[v] = ghi
        mc_lo[v] = glo

    H0, W0 = H // 4, W // 4
    PH0, PW0 = PH // 4, lanes(PW // 4)
    sum4[...] = select((iota((PW, PW0), 0) >> 2) == iota((PW, PW0), 1), 0.25)
    spread4[...] = select(
        ((iota((PW0, W), 1) + HC) >> 2) == iota((PW0, W), 0)
    )

    damp = jnp.full((1, 1), damping[0], F32)

    def apply_a(f, emit):
        for j in range(PW // BLK):
            cols = slice(BLK * j, BLK * j + BLK)
            xh, xl = split(fields[f, :, cols])
            t = dot(mr_hi[...], xh) + dot(mr_hi[...], xl) + dot(mr_lo[...], xh)
            th, tl = split(t)
            t_hi[:, cols] = th
            t_lo[:, cols] = tl
        for j in range(blocks):
            v = 0 if j == 0 else (2 if j == blocks - 1 else 1)
            win = slice(BLK * j, BLK * j + WIN)
            th, tl = t_hi[:, win], t_lo[:, win]
            mh, ml = mc_hi[v], mc_lo[v]
            x = fields[f, HR : HR + H, HC + BLK * j : HC + BLK * j + BLK]
            emit(j, x, dot(th, mh) + dot(tl, mh) + dot(th, ml) + damp * x)

    def put(f, j, value):
        fields[f, HR : HR + H, HC + BLK * j : HC + BLK * j + BLK] = value

    def plane_copy(e, i):
        return pltpu.make_async_remote_copy(
            src_ref=plane_sum.at[e, lin],
            dst_ref=plane_sum.at[e, lin],
            send_sem=psend_sem.at[e, i],
            recv_sem=precv_sem.at[e, i],
            device_id=device(slab, (lin + i) % n_lin),
            device_id_type=MESH,
        )

    def slab_copy(e, i):
        return pltpu.make_async_remote_copy(
            src_ref=slab_sum.at[e, slab],
            dst_ref=slab_sum.at[e, slab],
            send_sem=ssend_sem.at[e, i],
            recv_sem=srecv_sem.at[e, i],
            device_id=device((slab + i) % n_slab, lin),
            device_id_type=MESH,
        )

    def reduce_start(e, value):
        plane_sum[e, lin] = value
        for i in range(1, n_lin):
            plane_copy(e, i).start()

    def reduce_middle(e):
        for i in range(1, n_lin):
            plane_copy(e, i).wait_recv()
        total = plane_sum[e, 0]
        for i in range(1, n_lin):
            total = total + plane_sum[e, i]
        slab_sum[e, slab] = total
        for i in range(1, n_slab):
            slab_copy(e, i).start()

    def reduce_end(e):
        for i in range(1, n_slab):
            slab_copy(e, i).wait_recv()
        total = slab_sum[e, 0]
        for i in range(1, n_slab):
            total = total + slab_sum[e, i]
        return jnp.sum(total, axis=(0, 1), keepdims=True)

    loads[0].wait()
    halo_arrive(0, dir_in)
    parts = []

    def emit_q(j, x, y):
        put(2, j, y)
        parts.append(fold(x * y))

    apply_a(0, emit_q)
    halo_start(2)
    reduce_start(0, functools.reduce(jnp.add, parts))
    loads[1].wait()
    loads[2].wait()
    halo_arrive(1, res_in)
    reduce_middle(0)
    halo_arrive(2)
    rho_v = jnp.full((1, 1), rho[0], F32)
    alpha = rho_v / reduce_end(0)

    pick_rows = select((iota((PH0, PH), 1) >> 2) == iota((PH0, PH), 0))
    f0 = jnp.zeros((PH0, PW0), F32)
    for j in range(PW // BLK):
        cols = slice(BLK * j, BLK * j + BLK)
        r = fields[1, :, cols] - alpha * fields[2, :, cols]
        fields[1, :, cols] = r
        f0 = f0 + dot_right(dot_left(pick_rows, r), sum4[cols, :])
    res_copy = pltpu.make_async_copy(fields.at[1].at[centre], res_out, out_sem.at[0])
    res_copy.start()

    inv_diag = [RELAX / jnp.full((1, 1), diag[l], F32) for l in range(LEVELS)]

    def operator(l, v):
        return diag[l] * v - coupling[l] * beside(v)

    v0 = inv_diag[0] * f0
    t = f0 - operator(0, v0)
    rows = select((iota((H1, PH0), 1) - HR // 4) >> 1 == iota((H1, PH0), 0), 0.5)
    cols = select((iota((PW0, W1), 0) - HC // 4) >> 1 == iota((PW0, W1), 1))
    own_rows = pl.ds(pl.multiple_of(slab * H1, 8), H1)
    rhs1[own_rows, W1 : 2 * W1] = dot_right(dot_left(rows, t), cols)

    def gather_copy(dc, i):
        return pltpu.make_async_remote_copy(
            src_ref=rhs1.at[own_rows, pl.ds(W1, W1)],
            dst_ref=rhs1.at[own_rows, pl.ds(W1 - dc * W1, W1)],
            send_sem=gsend_sem.at[dc + 1, i],
            recv_sem=grecv_sem.at[dc + 1, i],
            device_id=device((slab + i) % n_slab, lin + dc),
            device_id_type=MESH,
        )

    def gather(action):
        for dc in (-1, 0, 1):
            for_recv = action == "wait_recv"

            @pl.when(exists(0, -dc if for_recv else dc))
            def _():
                for i in range(0 if dc else 1, n_slab):
                    getattr(gather_copy(dc, i), action)()

    gather("start")

    squares = []

    def emit_ar(j, x, y):
        put(3, j, y)
        squares.append((fold(x * x), fold(x * y), fold(y * y)))

    apply_a(1, emit_ar)
    halo_start(3)

    sol_buf[...] = sol_buf[...] + alpha * fields[0, HR : HR + H, HC : HC + W]
    sol_copy = pltpu.make_async_copy(sol_buf, sol_out, out_sem.at[1])
    sol_copy.start()

    gather("wait_recv")

    def level_shape(l):
        return (H1 * n_slab) >> (l - 1), lanes((3 * W1) >> (l - 1))

    def inside(l):
        shape = level_shape(l)
        width = W1 >> (l - 1)
        j = iota(shape, 1)
        column = j + (lin - 1) * width
        return (j < 3 * width) & (column >= 0) & (column < width * n_lin)

    def level(l, f):
        mask = inside(l)
        scale = inv_diag[l]
        v = scale * f
        if l == LEVELS - 1:
            for _ in range(COARSE_SWEEPS - 1):
                v = jnp.where(mask, v + scale * (f - operator(l, v)), 0.0)
            return v
        t = jnp.where(mask, f - operator(l, v), 0.0)
        (h, w), (hn, wn) = level_shape(l), level_shape(l + 1)
        down = select((iota((hn, h), 1) >> 1) == iota((hn, h), 0), 0.5)
        across = select((iota((w, wn), 0) >> 1) == iota((w, wn), 1))
        lower = level(l + 1, dot_right(dot_left(down, t), across))
        up = select((iota((h, hn), 0) >> 1) == iota((h, hn), 1))
        back = select((iota((wn, w), 1) >> 1) == iota((wn, w), 0))
        v = v + dot_left(up, dot_right(lower, back))
        return jnp.where(mask, v + scale * (f - operator(l, v)), 0.0)

    v1 = level(1, rhs1[...])
    R1, C1 = level_shape(1)
    up = select(((iota((PH0, R1), 0) + (slab * H0 - HR // 4)) >> 1) == iota((PH0, R1), 1))
    back = select(((iota((C1, PW0), 1) - HC // 4) >> 1) + W1 == iota((C1, PW0), 0))
    v0 = v0 + dot_right(dot_left(up, v1), back)
    v0 = v0 + inv_diag[0] * (f0 - operator(0, v0))
    i, j = iota((PH0, PW0), 0), iota((PH0, PW0), 1)
    own = (i >= HR // 4) & (i < HR // 4 + H0) & (j >= HC // 4) & (j < HC // 4 + W0)
    v0 = jnp.where(own, v0, 0.0)

    c = RELAX / (1.0 + damp)
    rr = functools.reduce(jnp.add, [s[0] for s in squares])
    ra = functools.reduce(jnp.add, [s[1] for s in squares])
    aa = functools.reduce(jnp.add, [s[2] for s in squares])
    reduce_start(
        1, 3.0 * c * rr - 3.0 * c * c * ra + c * c * c * aa + 4.0 * fold(f0 * v0)
    )

    up4 = select(((iota((H, PH0), 0) + HR) >> 2) == iota((H, PH0), 1))
    v0_hi, v0_lo = split(v0)
    wide_hi = dot(up4, v0_hi).astype(BF16)
    wide_lo = dot(up4, v0_lo).astype(BF16)

    halo_arrive(3)

    def emit_pre(j, x, y):
        cols = slice(BLK * j, BLK * j + BLK)
        r = fields[1, HR : HR + H, HC + BLK * j : HC + BLK * j + BLK]
        coarse = dot(wide_hi, spread4[:, cols]) + dot(wide_lo, spread4[:, cols])
        pre_buf[:, cols] = 3.0 * c * r - 3.0 * c * c * x + c * c * c * y + coarse

    apply_a(3, emit_pre)
    pre_copy = pltpu.make_async_copy(pre_buf, pre_out, out_sem.at[2])
    pre_copy.start()
    reduce_middle(1)
    energy = reduce_end(1)
    beta = energy / rho_v
    ndir_buf[...] = pre_buf[...] + beta * fields[0, HR : HR + H, HC : HC + W]
    ndir_copy = pltpu.make_async_copy(ndir_buf, ndir_out, out_sem.at[3])
    ndir_copy.start()
    energy_out[...] = energy

    halo_sent(0, dir_in)
    halo_sent(1, res_in)
    halo_sent(2)
    halo_sent(3)
    gather("wait_send")
    for e in range(2):
        for i in range(1, n_lin):
            plane_copy(e, i).wait_send()
        for i in range(1, n_slab):
            slab_copy(e, i).wait_send()
    res_copy.wait()
    sol_copy.wait()
    pre_copy.wait()
    ndir_copy.wait()


def solution(mesh):
    n_grp, n_slab, n_col = (mesh.shape[a] for a in ("grp", "slab", "col"))
    n_lin = n_grp * n_col

    def on_device(sol, res, direction, row_taps, col_taps, damping, rho, diag, coupling):
        H, W = sol.shape
        taps = row_taps.shape[0]
        PH, PW = H + 2 * HR, W + 2 * HC
        WIN = BLK + 2 * HC
        any_spec = pl.BlockSpec(memory_space=pl.ANY)
        smem = pl.BlockSpec(memory_space=pltpu.SMEM)
        vmem = pl.BlockSpec(memory_space=pltpu.VMEM)
        tile = jax.ShapeDtypeStruct((H, W), F32)
        dma = pltpu.SemaphoreType.DMA
        outs = pl.pallas_call(
            functools.partial(kernel, (H, W, n_slab, n_grp, n_col, taps)),
            out_shape=[tile] * 4 + [jax.ShapeDtypeStruct((1, 1), F32)],
            in_specs=[any_spec] * 3 + [smem] * 6,
            out_specs=[any_spec] * 4 + [vmem],
            scratch_shapes=[
                pltpu.VMEM((4, PH, PW), F32),
                pltpu.VMEM((WIN, WIN), F32),
                pltpu.VMEM((3, WIN, BLK), BF16),
                pltpu.VMEM((3, WIN, BLK), BF16),
                pltpu.VMEM((H, PH), BF16),
                pltpu.VMEM((H, PH), BF16),
                pltpu.VMEM((H, PW), BF16),
                pltpu.VMEM((H, PW), BF16),
                pltpu.VMEM((PW, lanes(PW // 4)), BF16),
                pltpu.VMEM((lanes(PW // 4), W), BF16),
                pltpu.VMEM((H, W), F32),
                pltpu.VMEM((H, W), F32),
                pltpu.VMEM((H, W), F32),
                pltpu.VMEM((H // 8 * n_slab, 3 * (W // 8)), F32),
                pltpu.VMEM((2, n_lin, 8, 128), F32),
                pltpu.VMEM((2, n_slab, 8, 128), F32),
                dma((3,)),
                dma((4,)),
                dma((4, 8)),
                dma((4, 8)),
                dma((3, n_slab)),
                dma((3, n_slab)),
                dma((2, n_lin)),
                dma((2, n_lin)),
                dma((2, n_slab)),
                dma((2, n_slab)),
            ],
            compiler_params=pltpu.CompilerParams(
                collective_id=0, has_side_effects=True, vmem_limit_bytes=48 * 1024 * 1024
            ),
        )(
            sol,
            res,
            direction,
            row_taps,
            col_taps,
            damping.reshape(1),
            rho.reshape(1),
            diag,
            coupling,
        )
        return (*outs[:4], outs[4].reshape(()))

    tile = P("slab", ("grp", "col"))
    return jax.shard_map(
        on_device,
        mesh=mesh,
        in_specs=(tile, tile, tile, P(), P(), P(), P(), P(), P()),
        out_specs=(tile, tile, tile, tile, P()),
        check_vma=False,
    )
```

profile of v0, /device:TPU:0, one launch (start us, length us, event | category | flops | bytes accessed | tf_op | source)
XLA Modules:
  0.0 53.5 jit_solution(12580971493459068733)
XLA Ops:
  1.3 0.0 copy-start.6
  1.9 0.0 copy-start.3
  2.0 0.0 copy-start.4
  2.0 0.0 copy-start.5
  2.0 0.0 copy-done.6
  2.0 0.6 %copy-done.3 = f32[31]{0:T(128)S(1)} copy-done((f32[31]{0:T(128)S(1)}, f32[31]{0:T(128)}, u32[]{:S(2)}) %copy-start.3) | copy-done | bytes 148
  2.6 0.0 copy-done.4
  2.6 0.0 copy-done.5
  2.6 0.0 copy-start
  2.6 1.0 %copy-done = f32[128,1024]{1,0:T(8,128)S(1)} copy-done((f32[128,1024]{1,0:T(8,128)S(1)}, f32[128,1024]{1,0:T(8,128)}, u32[]{:S(2)}) %copy-start) | copy-done | bytes 524312
  3.7 0.0 copy-start.1
  3.7 1.0 %copy-done.1 = f32[128,1024]{1,0:T(8,128)S(1)} copy-done((f32[128,1024]{1,0:T(8,128)S(1)}, f32[128,1024]{1,0:T(8,128)}, u32[]{:S(2)}) %copy-start.1) | copy-done | bytes 524312
  4.7 0.0 copy-start.2
  4.7 1.0 %copy-done.2 = f32[128,1024]{1,0:T(8,128)S(1)} copy-done((f32[128,1024]{1,0:T(8,128)S(1)}, f32[128,1024]{1,0:T(8,128)}, u32[]{:S(2)}) %copy-start.2) | copy-done | bytes 524312
  5.8 42.9 %shard_map.128 = (f32[128,1024]{1,0:T(8,128)S(1)}, f32[128,1024]{1,0:T(8,128)S(1)}, f32[128,1024]{1,0:T(8,128)S(1)}, f32[128,1024]{1,0:T(8,128)S(1)}, f32[1,1]{1,0:T(1,128)}) custom-call(f32[128,1024]{1,0:T(8,128)S(1)} %copy-done, f32[128,1024]{1,0:T(8,128)S(1)} %copy-done.1, f32[128,1024]{1,0:T(8,128)S(1)} %copy-done.2, f32[31]{0:T(128)S(1)} %copy-done.3, ...), custom_call_target="tpu_custom_call" | custom-call | tf_op jit(solution)/shard_map/pallas_call | solution.py:521
  48.7 0.8 %copy.21 = f32[128,1024]{1,0:T(8,128)} copy(f32[128,1024]{1,0:T(8,128)S(1)} %get-tuple-element.20) | data formatting | bytes 1048576
  49.5 0.8 %copy.22 = f32[128,1024]{1,0:T(8,128)} copy(f32[128,1024]{1,0:T(8,128)S(1)} %get-tuple-element.21) | data formatting | bytes 1048576
  50.3 0.8 %copy.23 = f32[128,1024]{1,0:T(8,128)} copy(f32[128,1024]{1,0:T(8,128)S(1)} %get-tuple-element.22) | data formatting | bytes 1048576
  51.0 0.8 %copy.24 = f32[128,1024]{1,0:T(8,128)} copy(f32[128,1024]{1,0:T(8,128)S(1)} %get-tuple-element.23) | data formatting | bytes 1048576
Async XLA Ops:
  1.3 0.7 %copy-start.6 = (f32[4]{0:T(128)S(1)}, f32[4]{0:T(128)}, u32[]{:S(2)}) copy-start(f32[4]{0:T(128)} %coupling.1) | copy-start | bytes 52
  1.9 0.7 %copy-start.3 = (f32[31]{0:T(128)S(1)}, f32[31]{0:T(128)}, u32[]{:S(2)}) copy-start(f32[31]{0:T(128)} %row_taps.1) | copy-start | bytes 376
  2.0 0.7 %copy-start.4 = (f32[31]{0:T(128)S(1)}, f32[31]{0:T(128)}, u32[]{:S(2)}) copy-start(f32[31]{0:T(128)} %col_taps.1) | copy-start | bytes 376
  2.0 0.7 %copy-start.5 = (f32[4]{0:T(128)S(1)}, f32[4]{0:T(128)}, u32[]{:S(2)}) copy-start(f32[4]{0:T(128)} %diag.1) | copy-start | bytes 52
  2.6 1.0 %copy-start = (f32[128,1024]{1,0:T(8,128)S(1)}, f32[128,1024]{1,0:T(8,128)}, u32[]{:S(2)}) copy-start(f32[128,1024]{1,0:T(8,128)} %sol_in.1) | copy-start | bytes 1572868
  3.7 1.0 %copy-start.1 = (f32[128,1024]{1,0:T(8,128)S(1)}, f32[128,1024]{1,0:T(8,128)}, u32[]{:S(2)}) copy-start(f32[128,1024]{1,0:T(8,128)} %res_in.1) | copy-start | bytes 1572868
  4.7 1.0 %copy-start.2 = (f32[128,1024]{1,0:T(8,128)S(1)}, f32[128,1024]{1,0:T(8,128)}, u32[]{:S(2)}) copy-start(f32[128,1024]{1,0:T(8,128)} %dir_in.1) | copy-start | bytes 1572868
where the time goes:
time: 53.8 us; the launch traced here: 53.5 us
  Pallas kernels  42.9 us (80%)
  local copies, waits for them, and re-layouts  6.95 us (13%)
  between operations  3.68 us (7%)
    pallas_call x1, Pallas kernels, on_device(): pl.pallas_call(functools.partial(kernel, (H, W, n_slab, n_grp, n_col, tap...  42.9 us
    unnamed x18, local copies, waits for them, and re-layouts  6.95 us

commit v1 on v0

--- a/solution.py
+++ b/solution.py
@@ -70,7 +70,6 @@
 
 def kernel(
     sizes,
-    sol_in,
     res_in,
     dir_in,
     row_taps,
@@ -79,10 +78,9 @@
     rho,
     diag,
     coupling,
-    sol_out,
     res_out,
     pre_out,
-    ndir_out,
+    alpha_out,
     energy_out,
     fields,
     band,
@@ -94,12 +92,9 @@
     t_lo,
     sum4,
     spread4,
-    sol_buf,
     pre_buf,
-    ndir_buf,
     rhs1,
-    plane_sum,
-    slab_sum,
+    parts_in,
     local_sem,
     out_sem,
     send_sem,
@@ -108,8 +103,6 @@
     grecv_sem,
     psend_sem,
     precv_sem,
-    ssend_sem,
-    srecv_sem,
 ):
     H, W, n_slab, n_grp, n_col, taps = sizes
     n_lin = n_grp * n_col
@@ -130,27 +123,23 @@
     loads = [
         pltpu.make_async_copy(dir_in, fields.at[0].at[centre], local_sem.at[0]),
         pltpu.make_async_copy(res_in, fields.at[1].at[centre], local_sem.at[1]),
-        pltpu.make_async_copy(sol_in, sol_buf, local_sem.at[2]),
     ]
     for load in loads:
         load.start()
 
     barrier = pltpu.get_barrier_semaphore()
-    for i in range(1, n_lin):
-        pl.semaphore_signal(
-            barrier, inc=1, device_id=device(slab, (lin + i) % n_lin), device_id_type=MESH
-        )
-    for dc in (-1, 0, 1):
-
-        @pl.when(exists(0, dc))
-        def _():
-            for i in range(1, n_slab):
-                pl.semaphore_signal(
-                    barrier,
-                    inc=1,
-                    device_id=device((slab + i) % n_slab, lin + dc),
-                    device_id_type=MESH,
-                )
+    count = n_slab * n_lin
+    me = slab * n_lin + lin
+
+    def other(i):
+        index = (me + i) % count
+        return device(index // n_lin, index % n_lin)
+
+    def greet(i, carry):
+        pl.semaphore_signal(barrier, inc=1, device_id=other(i), device_id_type=MESH)
+        return carry
+
+    lax.fori_loop(1, count, greet, 0)
 
     def side(d, halo, extent):
         return {-1: (0, halo), 0: (halo, extent), 1: (halo + extent, halo)}[d]
@@ -172,8 +161,7 @@
         def _():
             rhs1[:, c0 : c0 + W1] = jnp.zeros((H1 * n_slab, W1), F32)
 
-    near = 1 + (lin > 0).astype(jnp.int32) + (lin < n_lin - 1).astype(jnp.int32)
-    pl.semaphore_wait(barrier, n_lin - 1 + (n_slab - 1) * near)
+    pl.semaphore_wait(barrier, count - 1)
 
     def halo_copy(f, source, k):
         dz, dc = DIRS[k]
@@ -298,48 +286,30 @@
     def put(f, j, value):
         fields[f, HR : HR + H, HC + BLK * j : HC + BLK * j + BLK] = value
 
-    def plane_copy(e, i):
+    def part_copy(e, i, slot):
         return pltpu.make_async_remote_copy(
-            src_ref=plane_sum.at[e, lin],
-            dst_ref=plane_sum.at[e, lin],
+            src_ref=parts_in.at[e, me],
+            dst_ref=parts_in.at[e, slot],
             send_sem=psend_sem.at[e, i],
             recv_sem=precv_sem.at[e, i],
-            device_id=device(slab, (lin + i) % n_lin),
+            device_id=other(i),
             device_id_type=MESH,
         )
 
-    def slab_copy(e, i):
-        return pltpu.make_async_remote_copy(
-            src_ref=slab_sum.at[e, slab],
-            dst_ref=slab_sum.at[e, slab],
-            send_sem=ssend_sem.at[e, i],
-            recv_sem=srecv_sem.at[e, i],
-            device_id=device((slab + i) % n_slab, lin),
-            device_id_type=MESH,
-        )
+    def each(action):
+        def step(i, carry):
+            action(i)
+            return carry
+
+        lax.fori_loop(1, count, step, 0)
 
     def reduce_start(e, value):
-        plane_sum[e, lin] = value
-        for i in range(1, n_lin):
-            plane_copy(e, i).start()
-
-    def reduce_middle(e):
-        for i in range(1, n_lin):
-            plane_copy(e, i).wait_recv()
-        total = plane_sum[e, 0]
-        for i in range(1, n_lin):
-            total = total + plane_sum[e, i]
-        slab_sum[e, slab] = total
-        for i in range(1, n_slab):
-            slab_copy(e, i).start()
+        parts_in[e, me] = jnp.sum(value, axis=0, keepdims=True)
+        each(lambda i: part_copy(e, i, me).start())
 
     def reduce_end(e):
-        for i in range(1, n_slab):
-            slab_copy(e, i).wait_recv()
-        total = slab_sum[e, 0]
-        for i in range(1, n_slab):
-            total = total + slab_sum[e, i]
-        return jnp.sum(total, axis=(0, 1), keepdims=True)
+        each(lambda i: part_copy(e, i, me).wait_recv())
+        return jnp.sum(jnp.sum(parts_in[e], axis=0), axis=1, keepdims=True)
 
     loads[0].wait()
     halo_arrive(0, dir_in)
@@ -350,12 +320,10 @@
         parts.append(fold(x * y))
 
     apply_a(0, emit_q)
+    reduce_start(0, functools.reduce(jnp.add, parts))
     halo_start(2)
-    reduce_start(0, functools.reduce(jnp.add, parts))
     loads[1].wait()
-    loads[2].wait()
     halo_arrive(1, res_in)
-    reduce_middle(0)
     halo_arrive(2)
     rho_v = jnp.full((1, 1), rho[0], F32)
     alpha = rho_v / reduce_end(0)
@@ -411,10 +379,6 @@
 
     apply_a(1, emit_ar)
     halo_start(3)
-
-    sol_buf[...] = sol_buf[...] + alpha * fields[0, HR : HR + H, HC : HC + W]
-    sol_copy = pltpu.make_async_copy(sol_buf, sol_out, out_sem.at[1])
-    sol_copy.start()
 
     gather("wait_recv")
 
@@ -480,12 +444,8 @@
     apply_a(3, emit_pre)
     pre_copy = pltpu.make_async_copy(pre_buf, pre_out, out_sem.at[2])
     pre_copy.start()
-    reduce_middle(1)
     energy = reduce_end(1)
-    beta = energy / rho_v
-    ndir_buf[...] = pre_buf[...] + beta * fields[0, HR : HR + H, HC : HC + W]
-    ndir_copy = pltpu.make_async_copy(ndir_buf, ndir_out, out_sem.at[3])
-    ndir_copy.start()
+    alpha_out[...] = alpha
     energy_out[...] = energy
 
     halo_sent(0, dir_in)
@@ -494,14 +454,52 @@
     halo_sent(3)
     gather("wait_send")
     for e in range(2):
-        for i in range(1, n_lin):
-            plane_copy(e, i).wait_send()
-        for i in range(1, n_slab):
-            slab_copy(e, i).wait_send()
+        each(lambda i: part_copy(e, i, me).wait_send())
     res_copy.wait()
-    sol_copy.wait()
     pre_copy.wait()
-    ndir_copy.wait()
+
+
+def finish(
+    sol_in,
+    res_in,
+    pre_in,
+    dir_in,
+    alpha,
+    energy,
+    rho,
+    sol_out,
+    res_out,
+    pre_out,
+    ndir_out,
+    total_out,
+    sol,
+    res,
+    pre,
+    direction,
+    ndir,
+    load_sem,
+    store_sem,
+):
+    pairs = ((dir_in, direction), (sol_in, sol), (res_in, res), (pre_in, pre))
+    loads = [pltpu.make_async_copy(a, b, load_sem.at[i]) for i, (a, b) in enumerate(pairs)]
+    pairs = ((sol, sol_out), (res, res_out), (pre, pre_out), (ndir, ndir_out))
+    stores = [pltpu.make_async_copy(a, b, store_sem.at[i]) for i, (a, b) in enumerate(pairs)]
+    for load in loads:
+        load.start()
+    total_out[0] = energy[0, 0]
+    beta = jnp.full((1, 1), energy[0, 0], F32) / jnp.full((1, 1), rho[0], F32)
+    loads[0].wait()
+    loads[1].wait()
+    sol[...] = sol[...] + alpha[0, 0] * direction[...]
+    stores[0].start()
+    loads[2].wait()
+    stores[1].start()
+    loads[3].wait()
+    stores[2].start()
+    ndir[...] = pre[...] + beta * direction[...]
+    stores[3].start()
+    for store in stores:
+        store.wait()
 
 
 def solution(mesh):
@@ -518,11 +516,12 @@
         vmem = pl.BlockSpec(memory_space=pltpu.VMEM)
         tile = jax.ShapeDtypeStruct((H, W), F32)
         dma = pltpu.SemaphoreType.DMA
-        outs = pl.pallas_call(
+        rho = rho.reshape(1)
+        new_res, pre, alpha, energy = pl.pallas_call(
             functools.partial(kernel, (H, W, n_slab, n_grp, n_col, taps)),
-            out_shape=[tile] * 4 + [jax.ShapeDtypeStruct((1, 1), F32)],
-            in_specs=[any_spec] * 3 + [smem] * 6,
-            out_specs=[any_spec] * 4 + [vmem],
+            out_shape=[tile] * 2 + [jax.ShapeDtypeStruct((1, 1), F32)] * 2,
+            in_specs=[any_spec] * 2 + [smem] * 6,
+            out_specs=[any_spec] * 2 + [vmem] * 2,
             scratch_shapes=[
                 pltpu.VMEM((4, PH, PW), F32),
                 pltpu.VMEM((WIN, WIN), F32),
@@ -535,36 +534,38 @@
                 pltpu.VMEM((PW, lanes(PW // 4)), BF16),
                 pltpu.VMEM((lanes(PW // 4), W), BF16),
                 pltpu.VMEM((H, W), F32),
-                pltpu.VMEM((H, W), F32),
-                pltpu.VMEM((H, W), F32),
                 pltpu.VMEM((H // 8 * n_slab, 3 * (W // 8)), F32),
-                pltpu.VMEM((2, n_lin, 8, 128), F32),
-                pltpu.VMEM((2, n_slab, 8, 128), F32),
+                pltpu.VMEM((2, n_slab * n_lin, 1, 128), F32),
                 dma((3,)),
                 dma((4,)),
                 dma((4, 8)),
                 dma((4, 8)),
                 dma((3, n_slab)),
                 dma((3, n_slab)),
-                dma((2, n_lin)),
-                dma((2, n_lin)),
-                dma((2, n_slab)),
-                dma((2, n_slab)),
+                dma((2, n_slab * n_lin)),
+                dma((2, n_slab * n_lin)),
             ],
             compiler_params=pltpu.CompilerParams(
-                collective_id=0, has_side_effects=True, vmem_limit_bytes=48 * 1024 * 1024
+                collective_id=0, has_side_effects=True, vmem_limit_bytes=60 * 1024 * 1024
             ),
         )(
-            sol,
             res,
             direction,
             row_taps,
             col_taps,
             damping.reshape(1),
-            rho.reshape(1),
+            rho,
             diag,
             coupling,
         )
+        outs = pl.pallas_call(
+            finish,
+            out_shape=[tile] * 4 + [jax.ShapeDtypeStruct((1,), F32)],
+            in_specs=[any_spec] * 4 + [smem] * 3,
+            out_specs=[any_spec] * 4 + [smem],
+            scratch_shapes=[pltpu.VMEM((H, W), F32)] * 5 + [dma((4,)), dma((4,))],
+            compiler_params=pltpu.CompilerParams(vmem_limit_bytes=60 * 1024 * 1024),
+        )(sol, new_res, pre, direction, alpha, energy, rho)
         return (*outs[:4], outs[4].reshape(()))
 
     tile = P("slab", ("grp", "col"))

time: 53.8 us -> 46.3 us (0.86)
  local copies, waits for them, and re-layouts: 6.95 us -> 0 us
  between operations: 3.68 us -> 1.93 us
  Pallas kernels: 42.9 us -> 44.2 us
    unnamed x18 -> x0, local copies, waits for them, and re-layouts: 6.95 us -> none
    pallas_call x0 -> x1, Pallas kernels: none -> 4.34 us  [on_device(): pl.pallas_call(finish, out_shape=[tile] * 4 + [jax.ShapeDtypeStruct((1,),...]
    pallas_call x1, Pallas kernels: 42.9 us -> 39.8 us  [on_device(): pl.pallas_call(functools.partial(kernel, (H, W, n_slab, n_grp, n_col, tap...]
where the time goes in v1:
time: 46.3 us; the launch traced here: 46.1 us
  Pallas kernels  44.2 us (95%)
  between operations  1.93 us (4%)
    pallas_call x1, Pallas kernels, on_device(): pl.pallas_call(functools.partial(kernel, (H, W, n_slab, n_grp, n_col, tap...  39.8 us
    pallas_call x1, Pallas kernels, on_device(): pl.pallas_call(finish, out_shape=[tile] * 4 + [jax.ShapeDtypeStruct((1,),...  4.34 us

profile of v1, /device:TPU:0, one launch (start us, length us, event | category | flops | bytes accessed | tf_op | source)
XLA Modules:
  0.0 46.1 jit_solution(5797833108649702140)
XLA Ops:
  1.9 39.8 %shard_map.128 = (f32[128,1024]{1,0:T(8,128)}, f32[128,1024]{1,0:T(8,128)}, f32[1,1]{1,0:T(1,128)}, f32[1,1]{1,0:T(1,128)}) custom-call(f32[128,1024]{1,0:T(8,128)} %res_in.1, f32[128,1024]{1,0:T(8,128)} %dir_in.3, f32[31]{0:T(128)} %row_taps.1, f32[31]{0:T(128)} %col_taps.1, f32[1]{0:T(128)} %bitcast.3.damping, f32[1]{0:T(128)} %bitcast.4.rho, f32[4]{0:T(128)} %diag.1, ...), custom_call_target="tpu_custom_call" | custom-call | tf_op jit(solution)/shard_map/pallas_call | solution.py:520
  41.8 4.3 %shard_map.129 = (f32[128,1024]{1,0:T(8,128)}, f32[128,1024]{1,0:T(8,128)}, f32[128,1024]{1,0:T(8,128)}, f32[128,1024]{1,0:T(8,128)}, f32[1]{0:T(128)}) custom-call(f32[128,1024]{1,0:T(8,128)} %sol_in.1, f32[128,1024]{1,0:T(8,128)} %get-tuple-element.14.res_in, f32[128,1024]{1,0:T(8,128)} %get-tuple-element.15.pre_in, f32[128,1024]{1,0:T(8,128)} %dir_in.3, ...), custom_call_target="tpu_custom_call" | custom-call | tf_op jit(solution)/shard_map/pallas_call | solution.py:561

commit v2 on v1

--- a/solution.py
+++ b/solution.py
@@ -83,6 +83,8 @@
     alpha_out,
     energy_out,
     fields,
+    packed,
+    arrived,
     band,
     mc_hi,
     mc_lo,
@@ -111,8 +113,17 @@
     slab = lax.axis_index("slab")
     lin = lax.axis_index("grp") * n_col + lax.axis_index("col")
 
-    def device(s, l):
-        return (l // n_col, s, l % n_col)
+    grp, col = lax.axis_index("grp"), lax.axis_index("col")
+    at = {0: (grp, col)}
+    for dc in (-1, 1):
+        l = lin + dc + n_lin
+        at[dc] = (lax.rem(lax.div(l, n_col), n_grp), lax.rem(l, n_col))
+    grps = [lax.rem(grp + i, n_grp) for i in range(n_grp)]
+    slabs = [lax.rem(slab + i, n_slab) for i in range(n_slab)]
+    cols_of = [lax.rem(col + i, n_col) for i in range(n_col)]
+
+    def beside_device(s, dc):
+        return (at[dc][0], s, at[dc][1])
 
     def exists(dz, dc):
         s, l = slab + dz, lin + dc
@@ -131,27 +142,54 @@
     count = n_slab * n_lin
     me = slab * n_lin + lin
 
+    few = count <= 64
+
     def other(i):
-        index = (me + i) % count
-        return device(index // n_lin, index % n_lin)
-
-    def greet(i, carry):
-        pl.semaphore_signal(barrier, inc=1, device_id=other(i), device_id_type=MESH)
-        return carry
-
-    lax.fori_loop(1, count, greet, 0)
+        if few:
+            return (
+                grps[i // (n_slab * n_col)],
+                slabs[i // n_col % n_slab],
+                cols_of[i % n_col],
+            )
+        g = lax.div(i, n_slab * n_col)
+        rest = lax.rem(i, n_slab * n_col)
+        return (
+            lax.rem(grp + g, n_grp),
+            lax.rem(slab + lax.div(rest, n_col), n_slab),
+            lax.rem(col + lax.rem(rest, n_col), n_col),
+        )
+
+    def each(action):
+        if few:
+            for i in reversed(range(1, count)):
+                action(i)
+            return
+
+        def step(i, carry):
+            action(i)
+            return carry
+
+        lax.fori_loop(1, count, step, 0)
+
+    each(
+        lambda i: pl.semaphore_signal(
+            barrier, inc=1, device_id=other(i), device_id_type=MESH
+        )
+    )
 
     def side(d, halo, extent):
         return {-1: (0, halo), 0: (halo, extent), 1: (halo + extent, halo)}[d]
 
-    for dz, dc in DIRS:
-        r0, rn = side(dz, HR, H)
-        c0, cn = side(dc, HC, W)
-
-        @pl.when(jnp.logical_not(exists(dz, dc)))
+    for f in range(4):
+        for c0 in (0, HC + W):
+            fields[f, :, c0 : c0 + HC] = jnp.zeros((PH, HC), F32)
+    for dz in (-1, 1):
+        r0 = side(dz, HR, H)[0]
+
+        @pl.when(jnp.logical_not(exists(dz, 0)))
         def _():
             for f in range(4):
-                fields[f, r0 : r0 + rn, c0 : c0 + cn] = jnp.zeros((rn, cn), F32)
+                fields[f, r0 : r0 + HR, HC : HC + W] = jnp.zeros((HR, W), F32)
 
     W1 = W // 8
     H1 = H // 8
@@ -163,35 +201,78 @@
 
     pl.semaphore_wait(barrier, count - 1)
 
+    SIDE, CORNER = H // 4, HR // 4
+    EDGE = HC // 4
+    TOP, BOTTOM = slice(SIDE, SIDE + CORNER), slice(SIDE + CORNER, SIDE + 2 * CORNER)
+
+    def pack(f):
+        for i, c0 in enumerate((HC, HC + W - 128)):
+            first = 0 if i == 0 else 128 - EDGE
+            x = fields[f, HR : HR + H, c0 : c0 + 128][:, first : first + EDGE]
+
+            def groups(low, n):
+                return jnp.concatenate([x[low + n * g : low + n * g + n] for g in range(4)], axis=1)
+
+            packed[f, i, 0:SIDE] = groups(0, SIDE)
+            packed[f, i, TOP] = groups(0, CORNER)
+            packed[f, i, BOTTOM] = groups(H - HR, CORNER)
+
+    def unpack(f):
+        for i, c0 in enumerate((HC - EDGE, HC + W)):
+            dc = 2 * i - 1
+            for dz, r0, part, n in (
+                (0, HR, slice(0, SIDE), SIDE),
+                (-1, 0, TOP, CORNER),
+                (1, HR + H, BOTTOM, CORNER),
+            ):
+
+                @pl.when(exists(dz, dc))
+                def _():
+                    x = arrived[f, i, part]
+                    for g in range(4):
+                        fields[f, r0 + n * g : r0 + n * g + n, c0 : c0 + EDGE] = x[
+                            :, EDGE * g : EDGE * g + EDGE
+                        ]
+
     def halo_copy(f, source, k):
         dz, dc = DIRS[k]
-
-        def cut(d, halo, extent):
-            src = {-1: (0, halo), 0: (0, extent), 1: (extent - halo, halo)}[d]
-            dst = side(-d, halo, extent)[0]
-            return src[0], dst, src[1]
-
-        rs, rd, rn = cut(dz, HR, H)
-        cs, cd, cn = cut(dc, HC, W)
-        if source is None:
-            src = fields.at[f, pl.ds(HR + rs, rn), pl.ds(HC + cs, cn)]
+        if dc == 0:
+            rs = 0 if dz < 0 else H - HR
+            rd = HR + H if dz < 0 else 0
+            if source is None:
+                src = fields.at[f, pl.ds(HR + rs, HR), pl.ds(HC, W)]
+            else:
+                src = source.at[pl.ds(rs, HR), pl.ds(0, W)]
+            dst = fields.at[f, pl.ds(rd, HR), pl.ds(HC, W)]
         else:
-            src = source.at[pl.ds(rs, rn), pl.ds(cs, cn)]
+            i = 0 if dc < 0 else 1
+            low, n = {0: (0, SIDE), -1: (SIDE, CORNER), 1: (SIDE + CORNER, CORNER)}[dz]
+            land = {0: 0, -1: SIDE + CORNER, 1: SIDE}[dz]
+            src = packed.at[f, i, pl.ds(low, n)]
+            dst = arrived.at[f, 1 - i, pl.ds(land, n)]
         return pltpu.make_async_remote_copy(
             src_ref=src,
-            dst_ref=fields.at[f, pl.ds(rd, rn), pl.ds(cd, cn)],
+            dst_ref=dst,
             send_sem=send_sem.at[f, k],
             recv_sem=recv_sem.at[f, k],
-            device_id=device(slab + dz, lin + dc),
+            device_id=beside_device(slab + dz, dc),
             device_id_type=MESH,
         )
 
-    def halo_start(f, source=None):
-        for k, (dz, dc) in enumerate(DIRS):
-
-            @pl.when(exists(dz, dc))
-            def _():
-                halo_copy(f, source, k).start()
+    def halo_start(f, source=None, load=None):
+        def start(rows):
+            for k, (dz, dc) in enumerate(DIRS):
+                if (dc == 0) == rows:
+
+                    @pl.when(exists(dz, dc))
+                    def _():
+                        halo_copy(f, source, k).start()
+
+        start(True)
+        if load is not None:
+            load.wait()
+        pack(f)
+        start(False)
 
     def halo_arrive(f, source=None):
         for k, (dz, dc) in enumerate(DIRS):
@@ -200,6 +281,8 @@
             def _():
                 halo_copy(f, source, k).wait_recv()
 
+        unpack(f)
+
     def halo_sent(f, source=None):
         for k, (dz, dc) in enumerate(DIRS):
 
@@ -207,8 +290,8 @@
             def _():
                 halo_copy(f, source, k).wait_send()
 
-    halo_start(0, dir_in)
-    halo_start(1, res_in)
+    halo_start(0, dir_in, loads[0])
+    halo_start(1, res_in, loads[1])
 
     def banded(ref, first, rows, cols, offset):
         total = ref[0]
@@ -296,13 +379,6 @@
             device_id_type=MESH,
         )
 
-    def each(action):
-        def step(i, carry):
-            action(i)
-            return carry
-
-        lax.fori_loop(1, count, step, 0)
-
     def reduce_start(e, value):
         parts_in[e, me] = jnp.sum(value, axis=0, keepdims=True)
         each(lambda i: part_copy(e, i, me).start())
@@ -311,7 +387,6 @@
         each(lambda i: part_copy(e, i, me).wait_recv())
         return jnp.sum(jnp.sum(parts_in[e], axis=0), axis=1, keepdims=True)
 
-    loads[0].wait()
     halo_arrive(0, dir_in)
     parts = []
 
@@ -322,7 +397,6 @@
     apply_a(0, emit_q)
     reduce_start(0, functools.reduce(jnp.add, parts))
     halo_start(2)
-    loads[1].wait()
     halo_arrive(1, res_in)
     halo_arrive(2)
     rho_v = jnp.full((1, 1), rho[0], F32)
@@ -356,7 +430,7 @@
             dst_ref=rhs1.at[own_rows, pl.ds(W1 - dc * W1, W1)],
             send_sem=gsend_sem.at[dc + 1, i],
             recv_sem=grecv_sem.at[dc + 1, i],
-            device_id=device((slab + i) % n_slab, lin + dc),
+            device_id=beside_device(slabs[i], dc),
             device_id_type=MESH,
         )
 
@@ -524,6 +598,8 @@
             out_specs=[any_spec] * 2 + [vmem] * 2,
             scratch_shapes=[
                 pltpu.VMEM((4, PH, PW), F32),
+                pltpu.VMEM((4, 2, H // 4 + HR // 2, 128), F32),
+                pltpu.VMEM((4, 2, H // 4 + HR // 2, 128), F32),
                 pltpu.VMEM((WIN, WIN), F32),
                 pltpu.VMEM((3, WIN, BLK), BF16),
                 pltpu.VMEM((3, WIN, BLK), BF16),

time: 46.3 us -> 44.6 us (0.963)
  Pallas kernels: 44.2 us -> 42.5 us
    pallas_call x1, Pallas kernels: 39.8 us -> 38.1 us  [on_device(): pl.pallas_call(functools.partial(kernel, (H, W, n_slab, n_grp, n_col, tap...]
where the time goes in v2:
time: 44.6 us; the launch traced here: 44.4 us
  Pallas kernels  42.5 us (95%)
  between operations  1.93 us (4%)
    pallas_call x1, Pallas kernels, on_device(): pl.pallas_call(functools.partial(kernel, (H, W, n_slab, n_grp, n_col, tap...  38.1 us
    pallas_call x1, Pallas kernels, on_device(): pl.pallas_call(finish, out_shape=[tile] * 4 + [jax.ShapeDtypeStruct((1,),...  4.34 us

profile of v2, /device:TPU:0, one launch (start us, length us, event | category | flops | bytes accessed | tf_op | source)
XLA Modules:
  0.0 44.4 jit_solution(8586285977345868427)
XLA Ops:
  1.9 38.1 %shard_map.128 = (f32[128,1024]{1,0:T(8,128)}, f32[128,1024]{1,0:T(8,128)}, f32[1,1]{1,0:T(1,128)}, f32[1,1]{1,0:T(1,128)}) custom-call(f32[128,1024]{1,0:T(8,128)} %res_in.1, f32[128,1024]{1,0:T(8,128)} %dir_in.3, f32[31]{0:T(128)} %row_taps.1, f32[31]{0:T(128)} %col_taps.1, f32[1]{0:T(128)} %bitcast.3.damping, f32[1]{0:T(128)} %bitcast.4.rho, f32[4]{0:T(128)} %diag.1, ...), custom_call_target="tpu_custom_call" | custom-call | tf_op jit(solution)/shard_map/pallas_call | solution.py:594
  40.1 4.3 %shard_map.129 = (f32[128,1024]{1,0:T(8,128)}, f32[128,1024]{1,0:T(8,128)}, f32[128,1024]{1,0:T(8,128)}, f32[128,1024]{1,0:T(8,128)}, f32[1]{0:T(128)}) custom-call(f32[128,1024]{1,0:T(8,128)} %sol_in.1, f32[128,1024]{1,0:T(8,128)} %get-tuple-element.14.res_in, f32[128,1024]{1,0:T(8,128)} %get-tuple-element.15.pre_in, f32[128,1024]{1,0:T(8,128)} %dir_in.3, ...), custom_call_target="tpu_custom_call" | custom-call | tf_op jit(solution)/shard_map/pallas_call | solution.py:637
